TPU v7x, 128 devices: a whole 4x4x4 slice. The times are simulated.
128 devices in a mesh: tm: 8 (over z_lo, x), head: 16 (over y, z_hi, core).
Axes of the slice: x: 4, y: 4, z: 4 (z_hi: 2, z_lo: 2; z = z_hi * 2 + z_lo), core: 2. Of those that a mesh axis runs over, the one named last changes fastest.
Arguments:
- queries: bfloat16 [12288, 4096], P(('tm', 'head')), may hold values from -6 to 6
- key_tokens: bfloat16 [12288, 4096], P(('tm', 'head')), may hold values from -6 to 6
- value_tokens: bfloat16 [12288, 4096], P(('tm', 'head')), may hold values from -6 to 6
- outputs: bfloat16 [12288, 4096], P(('tm', 'head')), may hold values from -6 to 6
- out_grad: bfloat16 [12288, 4096], P(('tm', 'head')), may hold values from -96 to 96
- log_sum: float32 [12288, 32], P('tm', 'head'), may hold values from 7 to 9
- neighbours: int32 [96, 27], replicated, may hold values from -1 to 95, as said below
Outputs:
- query_grad: bfloat16 [12288, 4096], P(('tm', 'head'))
- key_grad: bfloat16 [12288, 4096], P(('tm', 'head'))
- value_grad: bfloat16 [12288, 4096], P(('tm', 'head'))
Inputs may be any that keep to these rules, and one draw needn't show every extreme that they name: `neighbours`: tile t lies in frame f = t // 12, tile row r and tile column c of that frame's grid of 3 x 4 tiles (rows major). Slot 9 a + 3 b + e of row t (a, b, e in 0, 1, 2) names the tile of frame f + a - 1, row r0 + b - 1, column c0 + e - 1, where the window centre (r0, c0) lies within one row and one column of (r, c) and the 3 x 3 window lies wholly inside the frame; the slot holds -1 exactly where frame f + a - 1 is outside the video.
All inputs are finite; a program needn't handle non-finite values.
Results may differ from a plain program's by a relative error of at most 0.0067.
Values may be sent and summed in bfloat16 or wider, within the bound.
A program may use at most 192 MiB of HBM per device.

v0:
```python
import jax
import jax.numpy as jnp
from jax import lax
from jax.sharding import PartitionSpec as P

HD = 128
TILE = 128


def padded(shard, sides, width):
    for axis, dim in sides:
        size, length = (lax.axis_size(axis), shard.shape[dim])
        up = [(i, (i + 1) % size) for i in range(size - 1)]
        down = [(j, i) for i, j in up]
        last = lax.slice_in_dim(shard, length - width, length, axis=dim)
        initial = lax.slice_in_dim(shard, 0, width, axis=dim)
        before = lax.ppermute(last, axis, up)
        after = lax.ppermute(initial, axis, down)
        shard = jnp.concatenate([before, shard, after], axis=dim)
    return shard


def head_delta(outs_in, grads_in):
    row_count, feat_width = outs_in.shape
    shaped = (row_count, feat_width // HD, HD)
    return jnp.sum(
        outs_in.reshape(shaped).astype(jnp.float32) * grads_in.reshape(shaped).astype(jnp.float32),
        axis=2,
    )


def as_tiles(source):
    return source.reshape((source.shape[0] // TILE, TILE) + source.shape[1:])


def both_rims(source, rim_rows, token_count):
    return jnp.concatenate([source[:rim_rows], source[rim_rows + token_count :]], 0)


def tile_grads(
    query_tiles,
    grad_tiles,
    stat_tiles,
    delta_tiles,
    slot_index,
    live_mask,
    kv_mask,
    key_buffer,
    value_buffer,
):
    tile_count, tile_len, feat_width = query_tiles.shape
    head_count = feat_width // HD
    buffer_count = key_buffer.shape[0]
    block_tiles = 4
    steps_total = tile_count // block_tiles
    block_rows = block_tiles * tile_len
    score_scale = HD ** (-0.5)
    buffer_ids = jnp.arange(buffer_count, dtype=jnp.int32)
    matches = (slot_index[:, :, None] == buffer_ids[None, None, :]).astype(jnp.float32)
    live_map = jnp.sum(matches * live_mask[:, :, None], axis=1)
    kv_map = jnp.sum(matches * kv_mask[:, :, None], axis=1)
    key_rows = key_buffer.reshape(buffer_count * tile_len, head_count, HD)
    value_rows = value_buffer.reshape(buffer_count * tile_len, head_count, HD)

    def to_blocks(source):
        return source.reshape((steps_total, block_rows) + source.shape[2:])

    def map_blocks(source):
        return source.reshape(steps_total, block_tiles, buffer_count)

    def expand(tile_map):
        return jnp.repeat(jnp.repeat(tile_map, tile_len, axis=0), tile_len, axis=1)

    def visit_block(totals, inputs):
        key_total, value_total = totals
        query_block, grad_block, stat_block, delta_block, live_block, kv_block = inputs
        query_heads = query_block.reshape(block_rows, head_count, HD)
        grad_heads = grad_block.reshape(block_rows, head_count, HD)
        live_tokens = expand(live_block)
        kv_tokens = expand(kv_block).astype(jnp.bfloat16)
        scores = (
            jnp.einsum("thd,shd->hts", query_heads, key_rows, preferred_element_type=jnp.float32)
            * score_scale
        )
        shifted = scores - stat_block.T[:, :, None]
        attn_weight = jnp.where(live_tokens[None] > 0, jnp.exp(jnp.minimum(shifted, 60.0)), 0.0)
        weight_low = attn_weight.astype(jnp.bfloat16)
        prob_grad = jnp.einsum(
            "thd,shd->hts", grad_heads, value_rows, preferred_element_type=jnp.float32
        )
        score_grad = (attn_weight * (prob_grad - delta_block.T[:, :, None])).astype(jnp.bfloat16)
        key_total = (
            key_total
            + jnp.einsum(
                "hts,thd->shd",
                score_grad * kv_tokens[None],
                query_heads,
                preferred_element_type=jnp.float32,
            )
            * score_scale
        )
        value_total = value_total + jnp.einsum(
            "hts,thd->shd",
            weight_low * kv_tokens[None],
            grad_heads,
            preferred_element_type=jnp.float32,
        )
        query_part = (
            jnp.einsum("hts,shd->thd", score_grad, key_rows, preferred_element_type=jnp.float32)
            * score_scale
        )
        return ((key_total, value_total), query_part.reshape(block_rows, feat_width))

    empty_sum = jnp.zeros((buffer_count * tile_len, head_count, HD), jnp.float32)
    inputs = (
        to_blocks(query_tiles),
        to_blocks(grad_tiles),
        to_blocks(stat_tiles),
        to_blocks(delta_tiles),
        map_blocks(live_map),
        map_blocks(kv_map),
    )
    totals, query_parts = lax.scan(visit_block, (empty_sum, empty_sum), inputs)
    query_parts = query_parts.reshape(tile_count, tile_len, feat_width)
    full_shape = (buffer_count, tile_len, feat_width)
    return (query_parts, totals[0].reshape(full_shape), totals[1].reshape(full_shape))


def shards(queries, key_tokens, value_tokens, outputs, out_grad, log_sum, neighbours):
    query_heads, key_heads, value_heads, output_heads, grad_heads = (
        lax.all_to_all(queries, "head", split_axis=1, concat_axis=0, tiled=True),
        lax.all_to_all(key_tokens, "head", split_axis=1, concat_axis=0, tiled=True),
        lax.all_to_all(value_tokens, "head", split_axis=1, concat_axis=0, tiled=True),
        lax.all_to_all(outputs, "head", split_axis=1, concat_axis=0, tiled=True),
        lax.all_to_all(out_grad, "head", split_axis=1, concat_axis=0, tiled=True),
    )
    delta_heads = head_delta(output_heads, grad_heads)
    token_count, feat_width = query_heads.shape
    tile_count = token_count // TILE
    first_tile = lax.axis_index("tm") * tile_count
    buffer_tiles = 3 * tile_count
    own_lists = lax.dynamic_slice_in_dim(neighbours, first_tile, tile_count, 0)
    own_live = (own_lists >= 0).astype(jnp.float32)
    own_slots = jnp.clip(own_lists - first_tile + tile_count, 0, buffer_tiles - 1)
    query_tiles = as_tiles(query_heads)
    grad_tiles = as_tiles(grad_heads)
    stat_tiles = as_tiles(log_sum)
    delta_tiles = as_tiles(delta_heads)
    extended = padded(jnp.stack([key_heads, value_heads]), (("tm", 1),), token_count)
    key_buffer = as_tiles(extended[0])
    value_buffer = as_tiles(extended[1])
    query_grad, key_sum, value_sum = tile_grads(
        query_tiles,
        grad_tiles,
        stat_tiles,
        delta_tiles,
        own_slots,
        own_live,
        own_live,
        key_buffer,
        value_buffer,
    )
    key_flat = key_sum.reshape(buffer_tiles * TILE, feat_width)
    value_flat = value_sum.reshape(buffer_tiles * TILE, feat_width)
    rim_terms = jnp.stack(
        [
            both_rims(key_flat, token_count, token_count),
            both_rims(value_flat, token_count, token_count),
        ]
    )
    arrived = padded(rim_terms, (("tm", 1),), token_count)
    central = jnp.stack(
        [key_flat[token_count : 2 * token_count], value_flat[token_count : 2 * token_count]]
    )
    central = central + arrived[:, :token_count] + arrived[:, 3 * token_count :]
    query_low = query_grad.reshape(token_count, feat_width).astype(jnp.bfloat16)
    key_low = central[0].astype(jnp.bfloat16)
    value_low = central[1].astype(jnp.bfloat16)
    result = (
        lax.all_to_all(query_low, "head", split_axis=0, concat_axis=1, tiled=True),
        lax.all_to_all(key_low, "head", split_axis=0, concat_axis=1, tiled=True),
        lax.all_to_all(value_low, "head", split_axis=0, concat_axis=1, tiled=True),
    )
    return (result[0], result[1], result[2])


def solution(mesh):
    placed = (
        P(("tm", "head"), None),
        P(("tm", "head"), None),
        P(("tm", "head"), None),
        P(("tm", "head"), None),
        P(("tm", "head"), None),
        P("tm", "head"),
        P(),
    )
    return jax.shard_map(
        shards,
        mesh=mesh,
        in_specs=placed,
        out_specs=(P(("tm", "head"), None), P(("tm", "head"), None), P(("tm", "head"), None)),
        check_vma=False,
    )
```

profile of v0, /device:TPU:43, one launch (start us, length us, event | category | flops | bytes accessed | tf_op | source)
XLA Modules:
  0.0 494.4 jit_solution(1179806800766683530)
XLA Ops:
  0.7 2.2 copy.220
  2.9 7.6 %all-to-all-start.1 = ((bf16[96,16,256]{2,0,1:T(8,128)(2,1)}), bf16[96,16,256]{2,0,1:T(8,128)(2,1)S(1)}, u32[]{:S(2)}, u32[]{:S(2)}) async-start(bf16[96,16,256]{2,0,1:T(8,128)(2,1)} %bitcast.106), calls=%async_computation.1 | async-start | bytes 1572864 | tf_op jit(solution)/shard_map/all_to_all | solution.py:132
  11.5 11.7 %all-to-all-done.1 = bf16[96,16,256]{2,0,1:T(8,128)(2,1)S(1)} async-done(((bf16[96,16,256]{2,0,1:T(8,128)(2,1)}), bf16[96,16,256]{2,0,1:T(8,128)(2,1)S(1)}, u32[]{:S(2)}, u32[]{:S(2)}) %all-to-all-start.1) | async-done | bytes 786464 | tf_op jit(solution)/shard_map/all_to_all | solution.py:132
  23.1 6.0 %all-to-all-start.2 = ((bf16[96,16,256]{2,0,1:T(8,128)(2,1)}), bf16[96,16,256]{2,0,1:T(8,128)(2,1)S(1)}, u32[]{:S(2)}, u32[]{:S(2)}) async-start(bf16[96,16,256]{2,0,1:T(8,128)(2,1)} %bitcast.105), calls=%async_computation.2 | async-start | bytes 1572864 | tf_op jit(solution)/shard_map/all_to_all | solution.py:133
  30.2 11.7 %all-to-all-done.2 = bf16[96,16,256]{2,0,1:T(8,128)(2,1)S(1)} async-done(((bf16[96,16,256]{2,0,1:T(8,128)(2,1)}), bf16[96,16,256]{2,0,1:T(8,128)(2,1)S(1)}, u32[]{:S(2)}, u32[]{:S(2)}) %all-to-all-start.2) | async-done | bytes 786464 | tf_op jit(solution)/shard_map/all_to_all | solution.py:133
  41.9 6.1 %all-to-all-start.4 = ((bf16[96,16,256]{2,0,1:T(8,128)(2,1)}), bf16[96,16,256]{2,0,1:T(8,128)(2,1)S(1)}, u32[]{:S(2)}, u32[]{:S(2)}) async-start(bf16[96,16,256]{2,0,1:T(8,128)(2,1)} %bitcast.103), calls=%async_computation.4 | async-start | bytes 1572864 | tf_op jit(solution)/shard_map/all_to_all | solution.py:134
  49.2 2.2 collective-permute-start.1
  51.4 3.1 collective-permute-start
  55.5 5.1 %all-to-all-done.4 = bf16[96,16,256]{2,0,1:T(8,128)(2,1)S(1)} async-done(((bf16[96,16,256]{2,0,1:T(8,128)(2,1)}), bf16[96,16,256]{2,0,1:T(8,128)(2,1)S(1)}, u32[]{:S(2)}, u32[]{:S(2)}) %all-to-all-start.4) | async-done | bytes 786464 | tf_op jit(solution)/shard_map/all_to_all | solution.py:134
  60.6 6.1 %all-to-all-start.3 = ((bf16[96,16,256]{2,0,1:T(8,128)(2,1)}), bf16[96,16,256]{2,0,1:T(8,128)(2,1)S(1)}, u32[]{:S(2)}, u32[]{:S(2)}) async-start(bf16[96,16,256]{2,0,1:T(8,128)(2,1)} %bitcast.104), calls=%async_computation.3 | async-start | bytes 1572864 | tf_op jit(solution)/shard_map/all_to_all | solution.py:135
  67.1 2.1 copy.221
  69.2 10.2 %all-to-all-done.3 = bf16[96,16,256]{2,0,1:T(8,128)(2,1)S(1)} async-done(((bf16[96,16,256]{2,0,1:T(8,128)(2,1)}), bf16[96,16,256]{2,0,1:T(8,128)(2,1)S(1)}, u32[]{:S(2)}, u32[]{:S(2)}) %all-to-all-start.3) | async-done | bytes 786464 | tf_op jit(solution)/shard_map/all_to_all | solution.py:135
  79.3 6.7 %all-to-all-start = ((bf16[96,16,256]{2,0,1:T(8,128)(2,1)}), bf16[96,16,256]{2,0,1:T(8,128)(2,1)}, u32[]{:S(2)}, u32[]{:S(2)}) async-start(bf16[96,16,256]{2,0,1:T(8,128)(2,1)} %bitcast.107), calls=%async_computation | async-start | bytes 1572864 | tf_op jit(solution)/shard_map/all_to_all | solution.py:131
  87.4 2.9 mul.66
  90.3 3.8 reduce_sum.20
  94.3 2.3 pad_maximum_fusion
  96.6 2.4 fusion.32
  99.0 2.8 copy.163
  101.9 2.4 copy.170
  104.3 4.3 copy.185
  108.6 209.8 %while.16 = (s32[]{:T(128)}, f32[4608,2,128]{0,2,1:T(8,128)}, f32[4608,2,128]{0,2,1:T(8,128)}, bf16[3,512,256]{2,1,0:T(8,128)(2,1)}, bf16[3,512,256]{2,1,0:T(8,1...) while((s32[]{:T(128)}, f32[4608,2,128]{0,2,1:T(8,128)}, ...), condition=%wide.region_3.4_spmd.clone, body=%wide.region_2.3_spmd.clone.sunk | while | flops 6112018432 | bytes 218225168 | solution.py:123
  112.4 4.6 copy.234
  117.0 2.5 broadcast_in_dim.96
  119.5 6.7 %copy.236 = bf16[512,4608]{1,0:T(8,128)(2,1)} copy(bf16[512,4608]{0,1:T(8,128)(2,1)} %bitcast.156) | data formatting | bytes 9437184 | tf_op jit(solution)/shard_map/while/body/eval_jaxpr/convert_element_type | solution.py:80
  126.2 9.6 %fusion.66 = f32[2,512,4608]{2,1,0:T(8,128)} fusion(bf16[512,2,128]{0,2,1:T(8,128)(2,1)S(1)} %bitcast.159, bf16[4608,2,128]{0,2,1:T(8,128)(2,1)} %get-tuple-element.347), kind=kOutput, calls=%fused_computation.55.clone.1 | convolution fusion | flops 1207959552 | bytes 21495808 | tf_op jit(solution)/shard_map/while/body/eval_jaxpr/thd,shd->hts/dot_general | solution.py:82
  135.8 13.6 %fusion.68 = f32[4608,2,128]{0,2,1:T(8,128)} fusion(bf16[512,2,128]{0,2,1:T(8,128)(2,1)S(1)} %bitcast.168, f32[2,512,4608]{2,1,0:T(8,128)} %fusion.66, f32[2,512]{1,0:T(2,128)S(1)} %get-tuple-element.310, pred[512,4608]{1,0:T(8,128)(4,1)} %copy.234, f32[4608,2,128]{0,2,1:T(8,128)} %get-tuple-element.328, bf16[512,4608]{1,0:T(8,128)(2,1)S(1)} %copy-done.2, ...), kind=kOutput, calls=%fused_computation.9.clone.1 | convolution fusion | flops 1238630400 | bytes 35655680 | tf_op jit(solution)/shard_map/while/body/eval_jaxpr/hts,thd->shd/dot_general | solution.py:102
  149.4 14.4 %multiply_convert_fusion.2 = bf16[2,512,4608]{2,1,0:T(8,128)(2,1)} fusion(f32[2,512,4608]{2,1,0:T(8,128)} %fusion.66, bf16[512,2,128]{0,2,1:T(8,128)(2,1)S(1)} %bitcast.169, bf16[4608,2,128]{2,0,1:T(8,128)(2,1)} %get-tuple-element.350, f32[2,512]{1,0:T(2,128)S(1)} %get-tuple-element.309, f32[2,512]{1,0:T(2,128)S(1)} %get-tuple-element.310, ...), kind=kOutput, calls=%fused_computation.clone.1 | convolution fusion | flops 1240989696 | bytes 33300480 | tf_op jit(solution)/shard_map/while/body/eval_jaxpr/thd,shd->hts/dot_general | solution.py:88
  163.8 9.4 %fusion.67 = f32[4608,2,128]{0,2,1:T(8,128)} fusion(bf16[512,2,128]{0,2,1:T(8,128)(2,1)S(1)} %bitcast.160, bf16[2,512,4608]{2,1,0:T(8,128)(2,1)} %multiply_convert_fusion.2, f32[4608,2,128]{0,2,1:T(8,128)} %get-tuple-element.327, bf16[512,4608]{1,0:T(8,128)(2,1)} %copy.236, pred[]{:T(512)S(6)} %compare.3), kind=kOutput, calls=%fused_computation.12.clone.1 | convolution fusion | flops 1216217088 | bytes 23855104 | tf_op jit(solution)/shard_map/while/body/eval_jaxpr/hts,thd->shd/dot_general | solution.py:94
  173.2 3.1 convolution_multiply_fusion.2
  180.9 4.6 copy.234
  185.5 2.5 broadcast_in_dim.96
  188.0 6.7 %copy.236 = bf16[512,4608]{1,0:T(8,128)(2,1)} copy(bf16[512,4608]{0,1:T(8,128)(2,1)} %bitcast.156) | data formatting | bytes 9437184 | tf_op jit(solution)/shard_map/while/body/eval_jaxpr/convert_element_type | solution.py:80
  194.7 9.6 %fusion.66 = f32[2,512,4608]{2,1,0:T(8,128)} fusion(bf16[512,2,128]{0,2,1:T(8,128)(2,1)S(1)} %bitcast.159, bf16[4608,2,128]{0,2,1:T(8,128)(2,1)} %get-tuple-element.347), kind=kOutput, calls=%fused_computation.55.clone.1 | convolution fusion | flops 1207959552 | bytes 21495808 | tf_op jit(solution)/shard_map/while/body/eval_jaxpr/thd,shd->hts/dot_general | solution.py:82
  204.3 14.3 %fusion.68 = f32[4608,2,128]{0,2,1:T(8,128)} fusion(bf16[512,2,128]{0,2,1:T(8,128)(2,1)S(1)} %bitcast.168, f32[2,512,4608]{2,1,0:T(8,128)} %fusion.66, f32[2,512]{1,0:T(2,128)S(1)} %get-tuple-element.310, pred[512,4608]{1,0:T(8,128)(4,1)} %copy.234, f32[4608,2,128]{0,2,1:T(8,128)} %get-tuple-element.328, bf16[512,4608]{1,0:T(8,128)(2,1)S(1)} %copy-done.2, ...), kind=kOutput, calls=%fused_computation.9.clone.1 | convolution fusion | flops 1238630400 | bytes 35655680 | tf_op jit(solution)/shard_map/while/body/eval_jaxpr/hts,thd->shd/dot_general | solution.py:102
  218.7 14.4 %multiply_convert_fusion.2 = bf16[2,512,4608]{2,1,0:T(8,128)(2,1)} fusion(f32[2,512,4608]{2,1,0:T(8,128)} %fusion.66, bf16[512,2,128]{0,2,1:T(8,128)(2,1)S(1)} %bitcast.169, bf16[4608,2,128]{2,0,1:T(8,128)(2,1)} %get-tuple-element.350, f32[2,512]{1,0:T(2,128)S(1)} %get-tuple-element.309, f32[2,512]{1,0:T(2,128)S(1)} %get-tuple-element.310, ...), kind=kOutput, calls=%fused_computation.clone.1 | convolution fusion | flops 1240989696 | bytes 33300480 | tf_op jit(solution)/shard_map/while/body/eval_jaxpr/thd,shd->hts/dot_general | solution.py:88
  233.1 10.8 %fusion.67 = f32[4608,2,128]{0,2,1:T(8,128)} fusion(bf16[512,2,128]{0,2,1:T(8,128)(2,1)S(1)} %bitcast.160, bf16[2,512,4608]{2,1,0:T(8,128)(2,1)} %multiply_convert_fusion.2, f32[4608,2,128]{0,2,1:T(8,128)} %get-tuple-element.327, bf16[512,4608]{1,0:T(8,128)(2,1)} %copy.236, pred[]{:T(512)S(6)} %compare.3), kind=kOutput, calls=%fused_computation.12.clone.1 | convolution fusion | flops 1216217088 | bytes 23855104 | tf_op jit(solution)/shard_map/while/body/eval_jaxpr/hts,thd->shd/dot_general | solution.py:94
  243.8 3.1 convolution_multiply_fusion.2
  251.5 4.6 copy.234
  256.1 2.5 broadcast_in_dim.96
  258.6 6.7 %copy.236 = bf16[512,4608]{1,0:T(8,128)(2,1)} copy(bf16[512,4608]{0,1:T(8,128)(2,1)} %bitcast.156) | data formatting | bytes 9437184 | tf_op jit(solution)/shard_map/while/body/eval_jaxpr/convert_element_type | solution.py:80
  265.3 9.6 %fusion.66 = f32[2,512,4608]{2,1,0:T(8,128)} fusion(bf16[512,2,128]{0,2,1:T(8,128)(2,1)S(1)} %bitcast.159, bf16[4608,2,128]{0,2,1:T(8,128)(2,1)} %get-tuple-element.347), kind=kOutput, calls=%fused_computation.55.clone.1 | convolution fusion | flops 1207959552 | bytes 21495808 | tf_op jit(solution)/shard_map/while/body/eval_jaxpr/thd,shd->hts/dot_general | solution.py:82
  275.0 14.3 %fusion.68 = f32[4608,2,128]{0,2,1:T(8,128)} fusion(bf16[512,2,128]{0,2,1:T(8,128)(2,1)S(1)} %bitcast.168, f32[2,512,4608]{2,1,0:T(8,128)} %fusion.66, f32[2,512]{1,0:T(2,128)S(1)} %get-tuple-element.310, pred[512,4608]{1,0:T(8,128)(4,1)} %copy.234, f32[4608,2,128]{0,2,1:T(8,128)} %get-tuple-element.328, bf16[512,4608]{1,0:T(8,128)(2,1)S(1)} %copy-done.2, ...), kind=kOutput, calls=%fused_computation.9.clone.1 | convolution fusion | flops 1238630400 | bytes 35655680 | tf_op jit(solution)/shard_map/while/body/eval_jaxpr/hts,thd->shd/dot_general | solution.py:102
  289.3 14.4 %multiply_convert_fusion.2 = bf16[2,512,4608]{2,1,0:T(8,128)(2,1)} fusion(f32[2,512,4608]{2,1,0:T(8,128)} %fusion.66, bf16[512,2,128]{0,2,1:T(8,128)(2,1)S(1)} %bitcast.169, bf16[4608,2,128]{2,0,1:T(8,128)(2,1)} %get-tuple-element.350, f32[2,512]{1,0:T(2,128)S(1)} %get-tuple-element.309, f32[2,512]{1,0:T(2,128)S(1)} %get-tuple-element.310, ...), kind=kOutput, calls=%fused_computation.clone.1 | convolution fusion | flops 1240989696 | bytes 33300480 | tf_op jit(solution)/shard_map/while/body/eval_jaxpr/thd,shd->hts/dot_general | solution.py:88
  303.7 10.8 %fusion.67 = f32[4608,2,128]{0,2,1:T(8,128)} fusion(bf16[512,2,128]{0,2,1:T(8,128)(2,1)S(1)} %bitcast.160, bf16[2,512,4608]{2,1,0:T(8,128)(2,1)} %multiply_convert_fusion.2, f32[4608,2,128]{0,2,1:T(8,128)} %get-tuple-element.327, bf16[512,4608]{1,0:T(8,128)(2,1)} %copy.236, pred[]{:T(512)S(6)} %compare.3), kind=kOutput, calls=%fused_computation.12.clone.1 | convolution fusion | flops 1216217088 | bytes 23855104 | tf_op jit(solution)/shard_map/while/body/eval_jaxpr/hts,thd->shd/dot_general | solution.py:94
  314.5 3.1 convolution_multiply_fusion.2
  318.4 6.9 %fusion.30 = (f32[1536,2,128]{0,2,1:T(8,128)S(1)}, f32[1536,2,128]{0,2,1:T(8,128)}, f32[1536,2,128]{0,2,1:T(8,128)}, f32[1536,2,128]{0,2,1:T(8,128)}, f32[1536,2,128]{0,2,1:T(8,128)}, /*index=5*/f32[1536,2,128]{0,2,1:T(8,128)S(1)}) fusion(f32[4608,2,128]{0,2,1:T(8,128)} %get-tuple-element.91, f32[4608,2,128]{0,2,1:T(8,128)} %get-tuple-element.92), kind=kLoop, calls=%fused_computation.51 | loop fusion | bytes 18874368 | tf_op jit(solution)/shard_map/slice | solution.py:173
  325.3 3.1 copy.191
  328.4 3.0 copy.190
  331.4 3.1 copy.192
  334.5 3.0 copy.193
  337.5 2.2 maximum_bitcast_fusion
  340.5 3.0 fusion.27
  343.6 3.1 collective-permute-start.2
  346.7 6.7 %collective-permute-start.3 = (f32[2,1536,256]{2,1,0:T(8,128)}, f32[2,1536,256]{2,1,0:T(8,128)}, u32[]{:S(2)}, u32[]{:S(2)}) collective-permute-start(f32[2,1536,256]{2,1,0:T(8,128)} %get-tuple-element.222), channel_id=1, source_target_pairs={{16,0},{32,16},{48,32},{64,48},{80,64},{96,80},{112,96},{17,1},{33... | collective-permute-start | bytes 9437192 | tf_op jit(solution)/shard_map/ppermute | solution.py:18
  353.4 8.1 %all-to-all-start.5 = ((bf16[16,96,256]{2,1,0:T(8,128)(2,1)}), bf16[16,96,256]{2,1,0:T(8,128)(2,1)}, u32[]{:S(2)}, u32[]{:S(2)}) async-start(bf16[16,96,256]{2,1,0:T(8,128)(2,1)} %bitcast.189), calls=%async_computation.5 | async-start | bytes 1572864 | tf_op jit(solution)/shard_map/all_to_all | solution.py:180
  361.5 1.6 copy.188
  363.1 1.6 copy.189
  364.8 53.8 %collective-permute-done.2 = f32[2,1536,256]{2,1,0:T(8,128)} collective-permute-done((f32[2,1536,256]{2,1,0:T(8,128)}, f32[2,1536,256]{2,1,0:T(8,128)}, u32[]{:S(2)}, u32[]{:S(2)}) %collective-permute-start.2) | collective-permute-done | bytes 3145760 | tf_op jit(solution)/shard_map/ppermute | solution.py:17
  418.6 31.1 %collective-permute-done.3 = f32[2,1536,256]{2,1,0:T(8,128)} collective-permute-done((f32[2,1536,256]{2,1,0:T(8,128)}, f32[2,1536,256]{2,1,0:T(8,128)}, u32[]{:S(2)}, u32[]{:S(2)}) %collective-permute-start.3) | collective-permute-done | bytes 3145760 | tf_op jit(solution)/shard_map/ppermute | solution.py:18
  449.7 3.8 fusion.29
  454.5 21.1 %all_to_all.125 = bf16[16,96,256]{2,1,0:T(8,128)(2,1)S(1)} all-to-all(bf16[16,96,256]{2,1,0:T(8,128)(2,1)S(1)} %bitcast.181), channel_id=1, replica_groups=mesh['tm'=8,'head'=16] {'head'}, dimensions={0} | all-to-all | bytes 1572864 | tf_op jit(solution)/shard_map/all_to_all | solution.py:181
  475.6 5.2 %all-to-all-start.7 = ((bf16[16,96,256]{2,1,0:T(8,128)(2,1)}), bf16[16,96,256]{2,1,0:T(8,128)(2,1)S(1)}, u32[]{:S(2)}, u32[]{:S(2)}) async-start(bf16[16,96,256]{2,1,0:T(8,128)(2,1)} %bitcast.25), calls=%async_computation.7 | async-start | bytes 1572864 | tf_op jit(solution)/shard_map/all_to_all | solution.py:182
  480.8 2.1 copy.209
  483.8 9.7 %all-to-all-done.7 = bf16[16,96,256]{2,1,0:T(8,128)(2,1)S(1)} async-done(((bf16[16,96,256]{2,1,0:T(8,128)(2,1)}), bf16[16,96,256]{2,1,0:T(8,128)(2,1)S(1)}, u32[]{:S(2)}, u32[]{:S(2)}) %all-to-all-start.7) | async-done | bytes 786464 | tf_op jit(solution)/shard_map/all_to_all | solution.py:182
  (114 shorter events, 23.6 us)
Async XLA Ops:
  0.6 66.0 %copy-start = (s32[96,27]{0,1:T(8,128)S(1)}, s32[96,27]{0,1:T(8,128)}, u32[]{:S(2)}) copy-start(s32[96,27]{0,1:T(8,128)} %param.15) | copy-start | bytes 31108
  0.6 9.9 %copy-start.9 = (bf16[96,4096]{1,0:T(8,128)(2,1)S(1)}, bf16[96,4096]{1,0:T(8,128)(2,1)}, u32[]{:S(2)}) copy-start(bf16[96,4096]{1,0:T(8,128)(2,1)} %param.11) | copy-start | bytes 2359300
  0.7 28.5 %copy-start.10 = (bf16[96,4096]{1,0:T(8,128)(2,1)S(1)}, bf16[96,4096]{1,0:T(8,128)(2,1)}, u32[]{:S(2)}) copy-start(bf16[96,4096]{1,0:T(8,128)(2,1)} %param.12) | copy-start | bytes 2359300
  2.9 20.3 %all-to-all-start.1 = ((bf16[96,16,256]{2,0,1:T(8,128)(2,1)}), bf16[96,16,256]{2,0,1:T(8,128)(2,1)S(1)}, u32[]{:S(2)}, u32[]{:S(2)}) async-start(bf16[96,16,256]{2,0,1:T(8,128)(2,1)} %bitcast.106), calls=%async_computation.1 | async-start | bytes 1572864 | tf_op jit(solution)/shard_map/all_to_all | solution.py:132
  23.1 18.7 %all-to-all-start.2 = ((bf16[96,16,256]{2,0,1:T(8,128)(2,1)}), bf16[96,16,256]{2,0,1:T(8,128)(2,1)S(1)}, u32[]{:S(2)}, u32[]{:S(2)}) async-start(bf16[96,16,256]{2,0,1:T(8,128)(2,1)} %bitcast.105), calls=%async_computation.2 | async-start | bytes 1572864 | tf_op jit(solution)/shard_map/all_to_all | solution.py:133
  29.2 25.3 %copy-start.11 = (bf16[96,4096]{1,0:T(8,128)(2,1)S(1)}, bf16[96,4096]{1,0:T(8,128)(2,1)}, u32[]{:S(2)}) copy-start(bf16[96,4096]{1,0:T(8,128)(2,1)} %param.13) | copy-start | bytes 2359300
  41.9 18.7 %all-to-all-start.4 = ((bf16[96,16,256]{2,0,1:T(8,128)(2,1)}), bf16[96,16,256]{2,0,1:T(8,128)(2,1)S(1)}, u32[]{:S(2)}, u32[]{:S(2)}) async-start(bf16[96,16,256]{2,0,1:T(8,128)(2,1)} %bitcast.103), calls=%async_computation.4 | async-start | bytes 1572864 | tf_op jit(solution)/shard_map/all_to_all | solution.py:134
  49.2 45.1 %collective-permute-start.1 = (bf16[2,1536,256]{2,1,0:T(8,128)(2,1)}, bf16[2,1536,256]{2,1,0:T(8,128)(2,1)}, u32[]{:S(2)}, u32[]{:S(2)}) collective-permute-start(bf16[2,1536,256]{2,1,0:T(8,128)(2,1)} %pad_maximum_fusion.2), channel_id=1, source_target_pairs={{16,0},{32,16},{48,32},{64,48},{80,64},{96,80},{112,96},{17,1},{33... | collective-permute-start | bytes 4718600 | tf_op jit(solution)/shard_map/ppermute | solution.py:18
  51.4 42.9 %collective-permute-start = (bf16[2,1536,256]{2,1,0:T(8,128)(2,1)}, bf16[2,1536,256]{2,1,0:T(8,128)(2,1)}, u32[]{:S(2)}, u32[]{:S(2)}) collective-permute-start(bf16[2,1536,256]{2,1,0:T(8,128)(2,1)} %pad_maximum_fusion.2), channel_id=1, source_target_pairs={{0,16},{16,32},{32,48},{48,64},{64,80},{80,96},{96,112},{1,17},{17... | collective-permute-start | bytes 4718600 | tf_op jit(solution)/shard_map/ppermute | solution.py:17
  60.6 18.7 %all-to-all-start.3 = ((bf16[96,16,256]{2,0,1:T(8,128)(2,1)}), bf16[96,16,256]{2,0,1:T(8,128)(2,1)S(1)}, u32[]{:S(2)}, u32[]{:S(2)}) async-start(bf16[96,16,256]{2,0,1:T(8,128)(2,1)} %bitcast.104), calls=%async_computation.3 | async-start | bytes 1572864 | tf_op jit(solution)/shard_map/all_to_all | solution.py:135
  79.3 29.3 %all-to-all-start = ((bf16[96,16,256]{2,0,1:T(8,128)(2,1)}), bf16[96,16,256]{2,0,1:T(8,128)(2,1)}, u32[]{:S(2)}, u32[]{:S(2)}) async-start(bf16[96,16,256]{2,0,1:T(8,128)(2,1)} %bitcast.107), calls=%async_computation | async-start | bytes 1572864 | tf_op jit(solution)/shard_map/all_to_all | solution.py:131
  126.2 9.6 %copy-start.2 = (bf16[512,4608]{1,0:T(8,128)(2,1)S(1)}, bf16[512,4608]{1,0:T(8,128)(2,1)}, u32[]{:S(2)}) copy-start(bf16[512,4608]{1,0:T(8,128)(2,1)} %copy.236) | copy-start | bytes 14155780 | tf_op jit(solution)/shard_map/while
  126.2 9.6 %copy-start.5 = (bf16[1,512,256]{1,2,0:T(8,128)(2,1)S(1)}, bf16[1,512,256]{1,2,0:T(8,128)(2,1)}, u32[]{:S(2)}) copy-start(bf16[1,512,256]{1,2,0:T(8,128)(2,1)} %copy.231) | copy-start | bytes 786436 | tf_op jit(solution)/shard_map/while
  163.8 9.4 %copy-start.3 = (bf16[2,512,4608]{2,1,0:T(8,128)(2,1)S(1)}, bf16[2,512,4608]{2,1,0:T(8,128)(2,1)}, u32[]{:S(2)}) copy-start(bf16[2,512,4608]{2,1,0:T(8,128)(2,1)} %multiply_convert_fusion.2) | copy-start | bytes 28311556 | tf_op jit(solution)/shard_map/while
  163.8 9.4 %copy-start.4 = (bf16[4608,2,128]{0,2,1:T(8,128)(2,1)S(1)}, bf16[4608,2,128]{0,2,1:T(8,128)(2,1)}, u32[]{:S(2)}) copy-start(bf16[4608,2,128]{0,2,1:T(8,128)(2,1)} %get-tuple-element.347) | copy-start | bytes 7077892 | tf_op jit(solution)/shard_map/while
  194.7 9.6 %copy-start.2 = (bf16[512,4608]{1,0:T(8,128)(2,1)S(1)}, bf16[512,4608]{1,0:T(8,128)(2,1)}, u32[]{:S(2)}) copy-start(bf16[512,4608]{1,0:T(8,128)(2,1)} %copy.236) | copy-start | bytes 14155780 | tf_op jit(solution)/shard_map/while
  194.7 9.6 %copy-start.5 = (bf16[1,512,256]{1,2,0:T(8,128)(2,1)S(1)}, bf16[1,512,256]{1,2,0:T(8,128)(2,1)}, u32[]{:S(2)}) copy-start(bf16[1,512,256]{1,2,0:T(8,128)(2,1)} %copy.231) | copy-start | bytes 786436 | tf_op jit(solution)/shard_map/while
  233.1 10.8 %copy-start.3 = (bf16[2,512,4608]{2,1,0:T(8,128)(2,1)S(1)}, bf16[2,512,4608]{2,1,0:T(8,128)(2,1)}, u32[]{:S(2)}) copy-start(bf16[2,512,4608]{2,1,0:T(8,128)(2,1)} %multiply_convert_fusion.2) | copy-start | bytes 28311556 | tf_op jit(solution)/shard_map/while
  233.1 10.8 %copy-start.4 = (bf16[4608,2,128]{0,2,1:T(8,128)(2,1)S(1)}, bf16[4608,2,128]{0,2,1:T(8,128)(2,1)}, u32[]{:S(2)}) copy-start(bf16[4608,2,128]{0,2,1:T(8,128)(2,1)} %get-tuple-element.347) | copy-start | bytes 7077892 | tf_op jit(solution)/shard_map/while
  265.3 9.6 %copy-start.2 = (bf16[512,4608]{1,0:T(8,128)(2,1)S(1)}, bf16[512,4608]{1,0:T(8,128)(2,1)}, u32[]{:S(2)}) copy-start(bf16[512,4608]{1,0:T(8,128)(2,1)} %copy.236) | copy-start | bytes 14155780 | tf_op jit(solution)/shard_map/while
  265.3 9.6 %copy-start.5 = (bf16[1,512,256]{1,2,0:T(8,128)(2,1)S(1)}, bf16[1,512,256]{1,2,0:T(8,128)(2,1)}, u32[]{:S(2)}) copy-start(bf16[1,512,256]{1,2,0:T(8,128)(2,1)} %copy.231) | copy-start | bytes 786436 | tf_op jit(solution)/shard_map/while
  303.7 10.8 %copy-start.3 = (bf16[2,512,4608]{2,1,0:T(8,128)(2,1)S(1)}, bf16[2,512,4608]{2,1,0:T(8,128)(2,1)}, u32[]{:S(2)}) copy-start(bf16[2,512,4608]{2,1,0:T(8,128)(2,1)} %multiply_convert_fusion.2) | copy-start | bytes 28311556 | tf_op jit(solution)/shard_map/while
  303.7 10.8 %copy-start.4 = (bf16[4608,2,128]{0,2,1:T(8,128)(2,1)S(1)}, bf16[4608,2,128]{0,2,1:T(8,128)(2,1)}, u32[]{:S(2)}) copy-start(bf16[4608,2,128]{0,2,1:T(8,128)(2,1)} %get-tuple-element.347) | copy-start | bytes 7077892 | tf_op jit(solution)/shard_map/while
  337.5 2.4 copy-start.6
  337.5 2.8 copy-start.7
  343.6 75.0 %collective-permute-start.2 = (f32[2,1536,256]{2,1,0:T(8,128)}, f32[2,1536,256]{2,1,0:T(8,128)}, u32[]{:S(2)}, u32[]{:S(2)}) collective-permute-start(f32[2,1536,256]{2,1,0:T(8,128)} %get-tuple-element.221), channel_id=1, source_target_pairs={{0,16},{16,32},{32,48},{48,64},{64,80},{80,96},{96,112},{1,17},{17... | collective-permute-start | bytes 9437192 | tf_op jit(solution)/shard_map/ppermute | solution.py:17
  346.7 103.0 %collective-permute-start.3 = (f32[2,1536,256]{2,1,0:T(8,128)}, f32[2,1536,256]{2,1,0:T(8,128)}, u32[]{:S(2)}, u32[]{:S(2)}) collective-permute-start(f32[2,1536,256]{2,1,0:T(8,128)} %get-tuple-element.222), channel_id=1, source_target_pairs={{16,0},{32,16},{48,32},{64,48},{80,64},{96,80},{112,96},{17,1},{33... | collective-permute-start | bytes 9437192 | tf_op jit(solution)/shard_map/ppermute | solution.py:18
  353.4 101.1 %all-to-all-start.5 = ((bf16[16,96,256]{2,1,0:T(8,128)(2,1)}), bf16[16,96,256]{2,1,0:T(8,128)(2,1)}, u32[]{:S(2)}, u32[]{:S(2)}) async-start(bf16[16,96,256]{2,1,0:T(8,128)(2,1)} %bitcast.189), calls=%async_computation.5 | async-start | bytes 1572864 | tf_op jit(solution)/shard_map/all_to_all | solution.py:180
  363.1 86.5 %copy-start.8 = (f32[1,1536,256]{2,1,0:T(8,128)S(1)}, f32[1,1536,256]{2,1,0:T(8,128)}, u32[]{:S(2)}) copy-start(f32[1,1536,256]{2,1,0:T(8,128)} %copy.188) | copy-start | bytes 4718596
  475.6 18.8 %copy-start.1 = (s32[96,27]{0,1:T(8,128)S(1)}, s32[96,27]{0,1:T(8,128)}, u32[]{:S(2)}) copy-start(s32[96,27]{0,1:T(8,128)} %param.15) | copy-start | bytes 31108
  475.6 17.9 %all-to-all-start.7 = ((bf16[16,96,256]{2,1,0:T(8,128)(2,1)}), bf16[16,96,256]{2,1,0:T(8,128)(2,1)S(1)}, u32[]{:S(2)}, u32[]{:S(2)}) async-start(bf16[16,96,256]{2,1,0:T(8,128)(2,1)} %bitcast.25), calls=%async_computation.7 | async-start | bytes 1572864 | tf_op jit(solution)/shard_map/all_to_all | solution.py:182
where the time goes:
time: 498 us; the launch traced here: 494 us
  matrix products  154 us (31%)
  waiting for transfers between devices  133 us (27%)
  local copies, waits for them, and re-layouts  106 us (21%)
  starting transfers between devices  60.8 us (12%)
  blocking collectives  21.1 us (4%)
  other arithmetic  18.2 us (4%)
    ppermute x2, waiting for transfers between devices, padded(): before = lax.ppermute(last, axis, up)  53.8 us
    dot_general x3, matrix products, visit_block(): jnp.einsum('thd,shd->hts', grad_heads, value_rows, preferred_element_type...  43.1 us
    dot_general x3, matrix products, visit_block(): jnp.einsum('hts,thd->shd', weight_low * kv_tokens[None], grad_heads, pref...  42.3 us
    ppermute x2, waiting for transfers between devices, padded(): after = lax.ppermute(initial, axis, down)  31.1 us
    dot_general x3, matrix products, visit_block(): jnp.einsum('hts,thd->shd', score_grad * kv_tokens[None], query_heads, pre...  30.9 us
    dot_general x3, matrix products, visit_block(): jnp.einsum('thd,shd->hts', query_heads, key_rows, preferred_element_type=...  28.8 us
    all_to_all x1, blocking collectives, shards(): lax.all_to_all(key_low, 'head', split_axis=0, concat_axis=1, tiled=True)  21.1 us
    convert_element_type x3, local copies, waits for them, and re-layouts, visit_block(): kv_tokens = expand(kv_block).astype(jnp.bfloat16)  20.1 us
  transfers between devices with their start and end apart: 11, of which 7 were waited for; matrix products, arithmetic and copies ran while one was open for 8% of the time, Pallas kernels for 0%

commit v1 on v0

v1 whole, which is shorter than its diff:
```python
import functools

import jax
import jax.numpy as jnp
from jax import lax
from jax.experimental import pallas as pl
from jax.experimental.pallas import tpu as pltpu
from jax.sharding import PartitionSpec as P

HD = 128
FRAME = 1536
SLAB = 96
ROWS = 3
QROW = 512
HEADS = 32
LOG2E = 1.4426950408889634
SCALE = HD**-0.5
MESH = pl.DeviceIdType.MESH
NT = (((1,), (1,)), ((), ()))
NN = (((1,), (0,)), ((), ()))


def dot(left, right, dims):
    return lax.dot_general(left, right, dims, preferred_element_type=jnp.float32)


def kernel(
    q_hbm, k_hbm, v_hbm, o_hbm, g_hbm, lse_hbm, bias,
    dq_out, dk_out, dv_out,
    qb, gb, kb, vb, kt, dqt, dka, dva, stat,
    ob, gl, dl_src, dl, ls, part_src, part, oq, ok, ov,
    load_sem, in_send, in_recv, halo_send, halo_recv, part_send, part_recv, out_send, out_recv,
):
    tm, hd = lax.axis_index("tm"), lax.axis_index("head")
    z_lo, x = tm // 4, tm % 4
    y, z_hi, core = hd // 4, (hd // 2) % 2, hd % 2
    place = 2 * (1 - z_lo) + core
    head = y * 8 + z_hi * 4 + x
    slot = tm % 2

    def holder(n):
        return ((1 - n // 2) * 4 + x, y * 4 + z_hi * 2 + n % 2)

    lower, upper = holder((place + 3) % 4), holder((place + 1) % 4)
    has_lower, has_upper = place > 0, place < 3

    def target(h):
        return ((1 - z_lo) * 4 + h % 4, (h // 8) * 4 + ((h // 4) % 2) * 2 + x // 2)

    def source(j, s):
        return (2 * place + j, s)

    load_o = pltpu.make_async_copy(o_hbm, ob, load_sem.at[0])
    load_g = pltpu.make_async_copy(g_hbm, gl, load_sem.at[1])
    load_o.start()
    load_g.start()

    barrier = pltpu.get_barrier_semaphore()

    def greet(i, _):
        pl.semaphore_signal(barrier, inc=1, device_id=source(i // 16, i % 16), device_id_type=MESH)
        return 0

    lax.fori_loop(0, 32, greet, 0)
    for peer in (lower, upper):
        pl.semaphore_signal(barrier, inc=1, device_id=peer, device_id_type=MESH)
    pl.semaphore_wait(barrier, 34)

    def columns(h):
        return pl.ds(pl.multiple_of(h * HD, HD), HD)

    first = (slot * 16 + hd) * 5

    def spread(array, src, dst, row):
        def send(i, _):
            h = (i + first) % HEADS
            pltpu.make_async_remote_copy(
                src.at[:, columns(h)],
                dst.at[pl.ds(pl.multiple_of(row, 32), SLAB)],
                in_send.at[array], in_recv.at[array, slot],
                device_id=target(h), device_id_type=MESH,
            ).start()
            return 0

        lax.fori_loop(0, HEADS, send, 0)

    own_row = (1 + slot) * FRAME + hd * SLAB
    kv_row = slot * FRAME + hd * SLAB
    spread(0, q_hbm, qb, own_row)
    spread(1, g_hbm, gb, own_row)
    for i in range(2):
        pltpu.make_async_remote_copy(
            lse_hbm.at[i], ls.at[1 + slot], in_send.at[5], in_recv.at[5, slot],
            device_id=target(2 * hd + i), device_id_type=MESH,
        ).start()
    spread(2, k_hbm, kb, kv_row)
    spread(3, v_hbm, vb, kv_row)

    load_o.wait()
    load_g.wait()

    def delta(h, _):
        product = ob[:, columns(h)].astype(jnp.float32) * gl[:, columns(h)].astype(jnp.float32)
        tall = jnp.concatenate([product, jnp.zeros((HD - SLAB, HD), jnp.float32)], axis=0)
        row = jnp.sum(tall.T, axis=0, keepdims=True)
        dl_src[h] = jnp.broadcast_to(row, (8, HD))
        return 0

    lax.fori_loop(0, HEADS, delta, 0)

    def send_delta(i, _):
        h = (i + first) % HEADS
        pltpu.make_async_remote_copy(
            dl_src.at[h], dl.at[1 + slot, hd], in_send.at[4], in_recv.at[4, slot],
            device_id=target(h), device_id_type=MESH,
        ).start()
        return 0

    lax.fori_loop(0, HEADS, send_delta, 0)

    def frame(ref, j):
        return ref.at[j * FRAME : (j + 1) * FRAME]

    kinds = (
        (0, lambda s: frame(qb, s)),
        (1, lambda s: frame(gb, s)),
        (4, lambda s: dl.at[s]),
        (5, lambda s: ls.at[s]),
    )

    def arrived(array, j, view):
        pltpu.make_async_remote_copy(
            view, view, in_send.at[array], in_recv.at[array, j], device_id=lower, device_id_type=MESH
        ).wait_recv()

    def halo(i, j, view):
        return pltpu.make_async_remote_copy(
            view(1 + j), view(3 - 3 * j), halo_send.at[i, j], halo_recv.at[i, j],
            device_id=upper if j else lower, device_id_type=MESH,
        )

    for i, (array, view) in enumerate(kinds):
        for j, has in ((0, has_lower), (1, has_upper)):
            arrived(array, j, view(1 + j))

            @pl.when(has)
            def _():
                halo(i, j, view).start()

    for j in range(2):
        arrived(2, j, frame(kb, j))
        arrived(3, j, frame(vb, j))

    for j in range(2):
        kt[:, j * FRAME : (j + 1) * FRAME] = (
            kb[j * FRAME : (j + 1) * FRAME, :].astype(jnp.float32).T.astype(jnp.bfloat16)
        )
    dqt[...] = jnp.zeros_like(dqt)
    dka[...] = jnp.zeros_like(dka)
    dva[...] = jnp.zeros_like(dva)

    for i, (array, view) in enumerate(kinds):

        @pl.when(has_upper)
        def _():
            pltpu.make_async_remote_copy(
                view(3), view(3), halo_send.at[i, 0], halo_recv.at[i, 0], device_id=lower, device_id_type=MESH
            ).wait_recv()

        @pl.when(has_lower)
        def _():
            pltpu.make_async_remote_copy(
                view(0), view(0), halo_send.at[i, 1], halo_recv.at[i, 1], device_id=upper, device_id_type=MESH
            ).wait_recv()

    lane = lax.broadcasted_iota(jnp.int32, (8, HD), 1)

    def make_stats(s):
        deltas = []
        for group in range(4):
            p0, p1, p2, p3 = (dl[s, 4 * group + i] for i in range(4))
            r1, r2, r3 = (pltpu.roll(p, 128 - 32 * i, 1) for i, p in ((1, p1), (2, p2), (3, p3)))
            deltas.append(jnp.where(lane < 96, p0, r1))
            deltas.append(jnp.where(lane < 64, r1, r2))
            deltas.append(jnp.where(lane < 32, r2, r3))
        for t in range(12):
            cols = slice((t % 4) * HD, (t % 4 + 1) * HD)
            lse = ls[s, t : t + 1, :] * LOG2E
            stat[s, t // 4, 0:1, cols] = lse
            stat[s, t // 4, 1:2, cols] = deltas[t][0:1, :]
            stat[s, t // 4, 2:3, cols] = lse + bias[s, 0, t : t + 1, :]
            stat[s, t // 4, 3:4, cols] = lse + bias[s, 1, t : t + 1, :]

    make_stats(1)
    make_stats(2)

    @pl.when(has_lower)
    def _():
        make_stats(0)

    @pl.when(has_upper)
    def _():
        make_stats(3)

    def block(i, _):
        pair, row = i // ROWS, i % ROWS
        j = pair // 3
        s = j + pair % 3
        at = pl.ds(pl.multiple_of(s * FRAME + row * QROW, QROW), QROW)
        keys = pl.ds(pl.multiple_of(j * FRAME, FRAME), FRAME)
        queries, grads = qb[at, :], gb[at, :]
        scores = dot(kb[keys, :], queries, NT)
        grad_p = dot(vb[keys, :], grads, NT)
        rest = stat[s, row, 1:2, :]
        weights, score_grads = [], []
        for t in range(12):
            band = slice(t * HD, (t + 1) * HD)
            which = (2, 0, 0, 3)[t % 4]
            weight = jnp.exp2(scores[band] * (SCALE * LOG2E) - stat[s, row, which : which + 1, :])
            weights.append(weight.astype(jnp.bfloat16))
            score_grads.append((weight * (grad_p[band] - rest)).astype(jnp.bfloat16))
        weights = jnp.concatenate(weights, axis=0)
        score_grads = jnp.concatenate(score_grads, axis=0)
        dva[keys, :] += dot(weights, grads, NN)
        dka[keys, :] += dot(score_grads, queries, NN)
        dqt[:, at] += dot(kt[:, keys], score_grads, NN)
        return 0

    lax.fori_loop(
        jnp.where(has_lower, 0, ROWS), jnp.where(has_upper, 6 * ROWS, 5 * ROWS), block, 0
    )

    def send_part(side):
        return pltpu.make_async_remote_copy(
            part_src.at[side], part.at[1 - side], part_send.at[side], part_recv.at[1 - side],
            device_id=upper if side else lower, device_id_type=MESH,
        )

    for side, has in ((0, has_lower), (1, has_upper)):

        @pl.when(has)
        def _():
            at = slice(3 * side * FRAME, (3 * side + 1) * FRAME)
            part_src[side] = dqt[:, at].T.astype(jnp.bfloat16)
            send_part(side).start()

    def gather(array, src, out):
        def send(i, _):
            piece = (i + 7 * head) % 32
            pltpu.make_async_remote_copy(
                src.at[pl.ds(pl.multiple_of(piece * SLAB, 32), SLAB)], out.at[:, columns(head)],
                out_send.at[array], out_recv.at[array],
                device_id=source(piece // 16, piece % 16), device_id_type=MESH,
            ).start()
            return 0

        lax.fori_loop(0, 32, send, 0)

    ok[...] = (dka[...] * SCALE).astype(jnp.bfloat16)
    gather(1, ok, dk_out)
    ov[...] = dva[...].astype(jnp.bfloat16)
    gather(2, ov, dv_out)

    for j, has in ((0, has_lower), (1, has_upper)):
        at = slice((1 + j) * FRAME, (2 + j) * FRAME)
        own = slice(j * FRAME, (j + 1) * FRAME)

        @pl.when(has)
        def _():
            pltpu.make_async_remote_copy(
                part.at[j], part.at[j], part_send.at[j], part_recv.at[j], device_id=lower, device_id_type=MESH
            ).wait_recv()
            oq[own, :] = ((dqt[:, at].T + part[j].astype(jnp.float32)) * SCALE).astype(jnp.bfloat16)

        @pl.when(jnp.logical_not(has))
        def _():
            oq[own, :] = (dqt[:, at].T * SCALE).astype(jnp.bfloat16)

    gather(0, oq, dq_out)

    for array, view in ((0, qb), (1, gb), (2, kb), (3, vb)):
        whole = view.at[0 : 2 * FRAME]
        pltpu.make_async_remote_copy(
            whole, whole, in_send.at[array], in_recv.at[array, 0], device_id=lower, device_id_type=MESH
        ).wait_send()
    pltpu.make_async_remote_copy(
        dl_src, dl_src, in_send.at[4], in_recv.at[4, 0], device_id=lower, device_id_type=MESH
    ).wait_send()
    pltpu.make_async_remote_copy(
        lse_hbm, lse_hbm, in_send.at[5], in_recv.at[5, 0], device_id=lower, device_id_type=MESH
    ).wait_send()
    for j, has in ((0, has_lower), (1, has_upper)):

        @pl.when(has)
        def _():
            for i, (array, view) in enumerate(kinds):
                halo(i, j, view).wait_send()
            send_part(j).wait_send()

    for array, src, out in ((0, oq, dq_out), (1, ok, dk_out), (2, ov, dv_out)):
        pltpu.make_async_remote_copy(
            src, src, out_send.at[array], out_recv.at[array], device_id=lower, device_id_type=MESH
        ).wait_send()
        pltpu.make_async_remote_copy(
            out, out, out_send.at[array], out_recv.at[array], device_id=lower, device_id_type=MESH
        ).wait_recv()


def shards(queries, key_tokens, value_tokens, outputs, out_grad, log_sum, neighbours):
    tm, hd = lax.axis_index("tm"), lax.axis_index("head")
    place = 2 * (1 - tm // 4) + hd % 2
    lse_rows = log_sum.T.reshape(2, 12, HD)
    centre = neighbours[:, 13] % 4
    hide = jnp.stack([centre == 2, centre == 1]).astype(jnp.float32) * 1e30
    hide = jnp.pad(hide, ((0, 0), (12, 12)))
    hide = lax.dynamic_slice_in_dim(hide, 24 * place, 48, 1).reshape(2, 4, 12)
    bias = jnp.broadcast_to(hide.transpose(1, 0, 2)[..., None], (4, 2, 12, HD))
    bf16, f32 = jnp.bfloat16, jnp.float32
    anywhere, vmem = pl.BlockSpec(memory_space=pl.ANY), pl.BlockSpec(memory_space=pltpu.VMEM)
    dma = pltpu.SemaphoreType.DMA
    token_shape = jax.ShapeDtypeStruct(queries.shape, bf16)
    return tuple(
        pl.pallas_call(
            kernel,
            out_shape=[token_shape] * 3,
            in_specs=[anywhere] * 6 + [vmem],
            out_specs=[anywhere] * 3,
            scratch_shapes=[
                pltpu.VMEM((4 * FRAME, HD), bf16),
                pltpu.VMEM((4 * FRAME, HD), bf16),
                pltpu.VMEM((2 * FRAME, HD), bf16),
                pltpu.VMEM((2 * FRAME, HD), bf16),
                pltpu.VMEM((HD, 2 * FRAME), bf16),
                pltpu.VMEM((HD, 4 * FRAME), f32),
                pltpu.VMEM((2 * FRAME, HD), f32),
                pltpu.VMEM((2 * FRAME, HD), f32),
                pltpu.VMEM((4, ROWS, 8, QROW), f32),
                pltpu.VMEM((SLAB, HEADS * HD), bf16),
                pltpu.VMEM((SLAB, HEADS * HD), bf16),
                pltpu.VMEM((HEADS, 8, HD), f32),
                pltpu.VMEM((4, 16, 8, HD), f32),
                pltpu.VMEM((4, 12, HD), f32),
                pltpu.VMEM((2, FRAME, HD), bf16),
                pltpu.VMEM((2, FRAME, HD), bf16),
                pltpu.VMEM((2 * FRAME, HD), bf16),
                pltpu.VMEM((2 * FRAME, HD), bf16),
                pltpu.VMEM((2 * FRAME, HD), bf16),
                dma((2,)),
                dma((6,)),
                dma((6, 2)),
                dma((4, 2)),
                dma((4, 2)),
                dma((2,)),
                dma((2,)),
                dma((3,)),
                dma((3,)),
            ],
            compiler_params=pltpu.CompilerParams(
                collective_id=0, has_side_effects=True, vmem_limit_bytes=60 << 20
            ),
        )(queries, key_tokens, value_tokens, outputs, out_grad, lse_rows, bias)
    )


def solution(mesh):
    tokens = P(("tm", "head"), None)
    return jax.shard_map(
        shards,
        mesh=mesh,
        in_specs=(tokens, tokens, tokens, tokens, tokens, P("tm", "head"), P()),
        out_specs=(tokens, tokens, tokens),
        check_vma=False,
    )
```

time: 498 us -> 136 us (0.27)
  the two profiles are of different devices: /device:TPU:43 before, /device:TPU:56 now
where the time goes in v1:
time: 136 us
  Pallas kernels  128 us (94%)
  local copies, waits for them, and re-layouts  6.44 us (5%)
    pallas_call x1, Pallas kernels, shards(): pl.pallas_call(kernel, out_shape=[token_shape] * 3, in_specs=[anywhere] *...  128 us
    unnamed x9, local copies, waits for them, and re-layouts  4.93 us

profile of v1, /device:TPU:56, one launch (start us, length us, event | category | flops | bytes accessed | tf_op | source)
XLA Modules:
  0.0 135.5 jit_solution(4688981358729229324)
XLA Ops:
  0.7 0.7 broadcast_compare_fusion.1
  1.4 0.0 copy-start.2
  1.4 0.1 pad_dynamic-slice_fusion
  1.5 0.1 reshape.82
  1.6 0.5 copy-done.2
  2.1 0.6 reshape.81.lse_hbm
  2.7 0.7 broadcast_in_dim.2.bias
  3.4 127.6 %shard_map.94 = (bf16[96,4096]{1,0:T(8,128)(2,1)}, bf16[96,4096]{1,0:T(8,128)(2,1)}, bf16[96,4096]{1,0:T(8,128)(2,1)}) custom-call(bf16[96,4096]{1,0:T(8,128)(2,1)} %q_hbm.1, bf16[96,4096]{1,0:T(8,128)(2,1)} %k_hbm.1, bf16[96,4096]{1,0:T(8,128)(2,1)} %v_hbm.1, bf16[96,4096]{1,0:T(8,128)(2,1)} %o_hbm.1, bf16[96,4096]{1,0:T(8,128)(2,1)} %g_hbm.1, ...), custom_call_target="tpu_custom_call" | custom-call | tf_op jit(solution)/shard_map/pallas_call | solution.py:323
  131.1 0.0 copy-start.1
  131.1 2.1 %copy.15 = bf16[96,4096]{1,0:T(8,128)(2,1)} copy(bf16[96,4096]{1,0:T(8,128)(2,1)} %get-tuple-element.8) | data formatting | bytes 1572864
  133.2 0.0 copy-done.1
  133.2 0.0 copy-start
  133.2 0.9 copy.16
  134.1 0.5 copy-done
  134.6 0.9 copy.17
  (3 shorter events, 0.0 us)
Async XLA Ops:
  1.4 0.7 copy-start.2
  131.1 2.1 %copy-start.1 = (bf16[96,4096]{1,0:T(8,128)(2,1)S(1)}, bf16[96,4096]{1,0:T(8,128)(2,1)}, u32[]{:S(2)}) copy-start(bf16[96,4096]{1,0:T(8,128)(2,1)} %get-tuple-element.9) | copy-start | bytes 2359300
  133.2 1.4 %copy-start = (bf16[96,4096]{1,0:T(8,128)(2,1)S(1)}, bf16[96,4096]{1,0:T(8,128)(2,1)}, u32[]{:S(2)}) copy-start(bf16[96,4096]{1,0:T(8,128)(2,1)} %get-tuple-element.10) | copy-start | bytes 2359300

commit v2 on v1

--- a/solution.py
+++ b/solution.py
@@ -27,7 +27,7 @@
 def kernel(
     q_hbm, k_hbm, v_hbm, o_hbm, g_hbm, lse_hbm, bias,
     dq_out, dk_out, dv_out,
-    qb, gb, kb, vb, kt, dqt, dka, dva, stat,
+    qb, gb, kb, vb, kt, dqt, dka, dva, stat, kept,
     ob, gl, dl_src, dl, ls, part_src, part, oq, ok, ov,
     load_sem, in_send, in_recv, halo_send, halo_recv, part_send, part_recv, out_send, out_recv,
 ):
@@ -87,14 +87,12 @@
     own_row = (1 + slot) * FRAME + hd * SLAB
     kv_row = slot * FRAME + hd * SLAB
     spread(0, q_hbm, qb, own_row)
-    spread(1, g_hbm, gb, own_row)
     for i in range(2):
         pltpu.make_async_remote_copy(
             lse_hbm.at[i], ls.at[1 + slot], in_send.at[5], in_recv.at[5, slot],
             device_id=target(2 * hd + i), device_id_type=MESH,
         ).start()
-    spread(2, k_hbm, kb, kv_row)
-    spread(3, v_hbm, vb, kv_row)
+    spread(1, g_hbm, gb, own_row)
 
     load_o.wait()
     load_g.wait()
@@ -121,61 +119,61 @@
     def frame(ref, j):
         return ref.at[j * FRAME : (j + 1) * FRAME]
 
-    kinds = (
-        (0, lambda s: frame(qb, s)),
-        (1, lambda s: frame(gb, s)),
-        (4, lambda s: dl.at[s]),
-        (5, lambda s: ls.at[s]),
-    )
+    kinds = {
+        0: lambda s: frame(qb, s),
+        1: lambda s: frame(gb, s),
+        4: lambda s: dl.at[s],
+        5: lambda s: ls.at[s],
+    }
 
     def arrived(array, j, view):
         pltpu.make_async_remote_copy(
             view, view, in_send.at[array], in_recv.at[array, j], device_id=lower, device_id_type=MESH
         ).wait_recv()
 
-    def halo(i, j, view):
+    def halo(array, j):
+        view = kinds[array]
         return pltpu.make_async_remote_copy(
-            view(1 + j), view(3 - 3 * j), halo_send.at[i, j], halo_recv.at[i, j],
+            view(1 + j), view(3 - 3 * j), halo_send.at[array, j], halo_recv.at[array, j],
             device_id=upper if j else lower, device_id_type=MESH,
         )
 
-    for i, (array, view) in enumerate(kinds):
-        for j, has in ((0, has_lower), (1, has_upper)):
-            arrived(array, j, view(1 + j))
+    sides = ((0, has_lower), (1, has_upper))
+
+    def forward(array):
+        for j, has in sides:
+            arrived(array, j, kinds[array](1 + j))
 
             @pl.when(has)
             def _():
-                halo(i, j, view).start()
-
-    for j in range(2):
-        arrived(2, j, frame(kb, j))
-        arrived(3, j, frame(vb, j))
-
-    for j in range(2):
-        kt[:, j * FRAME : (j + 1) * FRAME] = (
-            kb[j * FRAME : (j + 1) * FRAME, :].astype(jnp.float32).T.astype(jnp.bfloat16)
-        )
+                halo(array, j).start()
+
+    def halo_arrived(array):
+        for j, has in sides:
+
+            @pl.when(has)
+            def _():
+                view = kinds[array](3 * j)
+                pltpu.make_async_remote_copy(
+                    view, view, halo_send.at[array, 1 - j], halo_recv.at[array, 1 - j],
+                    device_id=lower, device_id_type=MESH,
+                ).wait_recv()
+
     dqt[...] = jnp.zeros_like(dqt)
     dka[...] = jnp.zeros_like(dka)
     dva[...] = jnp.zeros_like(dva)
 
-    for i, (array, view) in enumerate(kinds):
-
-        @pl.when(has_upper)
-        def _():
-            pltpu.make_async_remote_copy(
-                view(3), view(3), halo_send.at[i, 0], halo_recv.at[i, 0], device_id=lower, device_id_type=MESH
-            ).wait_recv()
-
-        @pl.when(has_lower)
-        def _():
-            pltpu.make_async_remote_copy(
-                view(0), view(0), halo_send.at[i, 1], halo_recv.at[i, 1], device_id=upper, device_id_type=MESH
-            ).wait_recv()
-
     lane = lax.broadcasted_iota(jnp.int32, (8, HD), 1)
 
-    def make_stats(s):
+    def lse_stats(s):
+        for t in range(12):
+            cols = slice((t % 4) * HD, (t % 4 + 1) * HD)
+            lse = ls[s, t : t + 1, :] * LOG2E
+            stat[s, t // 4, 0:1, cols] = lse
+            stat[s, t // 4, 2:3, cols] = lse + bias[s, 0, t : t + 1, :]
+            stat[s, t // 4, 3:4, cols] = lse + bias[s, 1, t : t + 1, :]
+
+    def delta_stats(s):
         deltas = []
         for group in range(4):
             p0, p1, p2, p3 = (dl[s, 4 * group + i] for i in range(4))
@@ -185,50 +183,57 @@
             deltas.append(jnp.where(lane < 32, r2, r3))
         for t in range(12):
             cols = slice((t % 4) * HD, (t % 4 + 1) * HD)
-            lse = ls[s, t : t + 1, :] * LOG2E
-            stat[s, t // 4, 0:1, cols] = lse
             stat[s, t // 4, 1:2, cols] = deltas[t][0:1, :]
-            stat[s, t // 4, 2:3, cols] = lse + bias[s, 0, t : t + 1, :]
-            stat[s, t // 4, 3:4, cols] = lse + bias[s, 1, t : t + 1, :]
-
-    make_stats(1)
-    make_stats(2)
-
-    @pl.when(has_lower)
-    def _():
-        make_stats(0)
-
-    @pl.when(has_upper)
-    def _():
-        make_stats(3)
-
-    def block(i, _):
-        pair, row = i // ROWS, i % ROWS
-        j = pair // 3
-        s = j + pair % 3
-        at = pl.ds(pl.multiple_of(s * FRAME + row * QROW, QROW), QROW)
-        keys = pl.ds(pl.multiple_of(j * FRAME, FRAME), FRAME)
-        queries, grads = qb[at, :], gb[at, :]
-        scores = dot(kb[keys, :], queries, NT)
-        grad_p = dot(vb[keys, :], grads, NT)
-        rest = stat[s, row, 1:2, :]
-        weights, score_grads = [], []
+
+    def at_rows(s, row):
+        return pl.ds(pl.multiple_of(s * FRAME + row * QROW, QROW), QROW)
+
+    def at_keys(j):
+        return pl.ds(pl.multiple_of(j * FRAME, FRAME), FRAME)
+
+    def at_kept(j, s):
+        return pl.ds(pl.multiple_of((2 * j + s) * FRAME, FRAME), FRAME)
+
+    def at_lanes(row):
+        return pl.ds(pl.multiple_of(row * QROW, QROW), QROW)
+
+    def weigh(j, s, row):
+        scores = dot(kb[at_keys(j), :], qb[at_rows(s, row), :], NT)
+        weights = []
         for t in range(12):
-            band = slice(t * HD, (t + 1) * HD)
             which = (2, 0, 0, 3)[t % 4]
-            weight = jnp.exp2(scores[band] * (SCALE * LOG2E) - stat[s, row, which : which + 1, :])
-            weights.append(weight.astype(jnp.bfloat16))
-            score_grads.append((weight * (grad_p[band] - rest)).astype(jnp.bfloat16))
-        weights = jnp.concatenate(weights, axis=0)
-        score_grads = jnp.concatenate(score_grads, axis=0)
-        dva[keys, :] += dot(weights, grads, NN)
-        dka[keys, :] += dot(score_grads, queries, NN)
-        dqt[:, at] += dot(kt[:, keys], score_grads, NN)
-        return 0
-
-    lax.fori_loop(
-        jnp.where(has_lower, 0, ROWS), jnp.where(has_upper, 6 * ROWS, 5 * ROWS), block, 0
-    )
+            shifted = scores[t * HD : (t + 1) * HD] * (SCALE * LOG2E) - stat[s, row, which : which + 1, :]
+            weights.append(jnp.exp2(shifted).astype(jnp.bfloat16))
+        kept[at_kept(j, s), at_lanes(row)] = jnp.concatenate(weights, axis=0)
+
+    def value_terms(j, s):
+        grads = gb[pl.ds(pl.multiple_of(s * FRAME, FRAME), FRAME), :]
+        dva[at_keys(j), :] += dot(kept[at_kept(j, s), :], grads, NN)
+
+    def score_terms(j, s, row):
+        queries = qb[at_rows(s, row), :]
+        grad_p = dot(vb[at_keys(j), :], gb[at_rows(s, row), :], NT)
+        weights = kept[at_kept(j, s), at_lanes(row)].astype(jnp.float32)
+        score_grads = (weights * (grad_p - stat[s, row, 1:2, :])).astype(jnp.bfloat16)
+        dka[at_keys(j), :] += dot(score_grads, queries, NN)
+        dqt[:, at_rows(s, row)] += dot(kt[:, at_keys(j)], score_grads, NN)
+
+    def each(count, step):
+        def body(i, _):
+            step(i)
+            return 0
+
+        lax.fori_loop(0, count, body, 0)
+
+    def on_halo(step):
+        for j, has in sides:
+
+            @pl.when(has)
+            def _():
+                step(j, 3 * j)
+
+    def on_rows(term, j, s):
+        each(ROWS, lambda row: term(j, s, row))
 
     def send_part(side):
         return pltpu.make_async_remote_copy(
@@ -236,47 +241,89 @@
             device_id=upper if side else lower, device_id_type=MESH,
         )
 
-    for side, has in ((0, has_lower), (1, has_upper)):
-
-        @pl.when(has)
-        def _():
-            at = slice(3 * side * FRAME, (3 * side + 1) * FRAME)
-            part_src[side] = dqt[:, at].T.astype(jnp.bfloat16)
-            send_part(side).start()
-
-    def gather(array, src, out):
-        def send(i, _):
-            piece = (i + 7 * head) % 32
+    def gather(array, j, src, out):
+        def send(i):
+            piece = (i + head) % 16
             pltpu.make_async_remote_copy(
-                src.at[pl.ds(pl.multiple_of(piece * SLAB, 32), SLAB)], out.at[:, columns(head)],
+                src.at[pl.ds(pl.multiple_of(j * FRAME + piece * SLAB, 32), SLAB)], out.at[:, columns(head)],
                 out_send.at[array], out_recv.at[array],
-                device_id=source(piece // 16, piece % 16), device_id_type=MESH,
+                device_id=source(j, piece), device_id_type=MESH,
             ).start()
-            return 0
-
-        lax.fori_loop(0, 32, send, 0)
-
-    ok[...] = (dka[...] * SCALE).astype(jnp.bfloat16)
-    gather(1, ok, dk_out)
-    ov[...] = dva[...].astype(jnp.bfloat16)
-    gather(2, ov, dv_out)
-
-    for j, has in ((0, has_lower), (1, has_upper)):
+
+        each(16, send)
+
+    def own(j):
+        return slice(j * FRAME, (j + 1) * FRAME)
+
+    def finish_keys(j):
+        ok[own(j), :] = (dka[own(j), :] * SCALE).astype(jnp.bfloat16)
+        gather(1, j, ok, dk_out)
+
+    def finish_queries(j, has):
         at = slice((1 + j) * FRAME, (2 + j) * FRAME)
-        own = slice(j * FRAME, (j + 1) * FRAME)
 
         @pl.when(has)
         def _():
             pltpu.make_async_remote_copy(
                 part.at[j], part.at[j], part_send.at[j], part_recv.at[j], device_id=lower, device_id_type=MESH
             ).wait_recv()
-            oq[own, :] = ((dqt[:, at].T + part[j].astype(jnp.float32)) * SCALE).astype(jnp.bfloat16)
+            oq[own(j), :] = ((dqt[:, at].T + part[j].astype(jnp.float32)) * SCALE).astype(jnp.bfloat16)
 
         @pl.when(jnp.logical_not(has))
         def _():
-            oq[own, :] = (dqt[:, at].T * SCALE).astype(jnp.bfloat16)
-
-    gather(0, oq, dq_out)
+            oq[own(j), :] = (dqt[:, at].T * SCALE).astype(jnp.bfloat16)
+
+        gather(0, j, oq, dq_out)
+
+    forward(0)
+    forward(5)
+    spread(2, k_hbm, kb, kv_row)
+    forward(1)
+    forward(4)
+    spread(3, v_hbm, vb, kv_row)
+    lse_stats(1)
+    lse_stats(2)
+    for j in range(2):
+        arrived(2, j, frame(kb, j))
+    each(12, lambda i: weigh(i // 6, 1 + i // 3 % 2, i % 3))
+    halo_arrived(0)
+    halo_arrived(5)
+
+    def halo_weights(j, s):
+        lse_stats(s)
+        on_rows(weigh, j, s)
+
+    on_halo(halo_weights)
+    for j in range(2):
+        kt[:, own(j)] = kb[own(j), :].astype(jnp.float32).T.astype(jnp.bfloat16)
+
+    delta_stats(1)
+    delta_stats(2)
+    each(4, lambda i: value_terms(i // 2, 1 + i % 2))
+    halo_arrived(1)
+    halo_arrived(4)
+    on_halo(value_terms)
+    ov[...] = dva[...].astype(jnp.bfloat16)
+    gather(2, 0, ov, dv_out)
+
+    for j in range(2):
+        arrived(3, j, frame(vb, j))
+
+    def halo_scores(j, s):
+        delta_stats(s)
+        on_rows(score_terms, j, s)
+        part_src[j] = dqt[:, s * FRAME : (s + 1) * FRAME].T.astype(jnp.bfloat16)
+        send_part(j).start()
+
+    on_halo(halo_scores)
+    gather(2, 1, ov, dv_out)
+    each(6, lambda i: score_terms(0, 1 + i // 3, i % 3))
+    finish_keys(0)
+    on_rows(score_terms, 1, 1)
+    finish_queries(0, has_lower)
+    on_rows(score_terms, 1, 2)
+    finish_keys(1)
+    finish_queries(1, has_upper)
 
     for array, view in ((0, qb), (1, gb), (2, kb), (3, vb)):
         whole = view.at[0 : 2 * FRAME]
@@ -293,8 +340,8 @@
 
         @pl.when(has)
         def _():
-            for i, (array, view) in enumerate(kinds):
-                halo(i, j, view).wait_send()
+            for array in kinds:
+                halo(array, j).wait_send()
             send_part(j).wait_send()
 
     for array, src, out in ((0, oq, dq_out), (1, ok, dk_out), (2, ov, dv_out)):
@@ -335,6 +382,7 @@
                 pltpu.VMEM((2 * FRAME, HD), f32),
                 pltpu.VMEM((2 * FRAME, HD), f32),
                 pltpu.VMEM((4, ROWS, 8, QROW), f32),
+                pltpu.VMEM((6 * FRAME, FRAME), bf16),
                 pltpu.VMEM((SLAB, HEADS * HD), bf16),
                 pltpu.VMEM((SLAB, HEADS * HD), bf16),
                 pltpu.VMEM((HEADS, 8, HD), f32),
@@ -348,15 +396,15 @@
                 dma((2,)),
                 dma((6,)),
                 dma((6, 2)),
-                dma((4, 2)),
-                dma((4, 2)),
+                dma((6, 2)),
+                dma((6, 2)),
                 dma((2,)),
                 dma((2,)),
                 dma((3,)),
                 dma((3,)),
             ],
             compiler_params=pltpu.CompilerParams(
-                collective_id=0, has_side_effects=True, vmem_limit_bytes=60 << 20
+                collective_id=0, has_side_effects=True, vmem_limit_bytes=67043328
             ),
         )(queries, key_tokens, value_tokens, outputs, out_grad, lse_rows, bias)
     )

time: 136 us -> 121 us (0.89)
  the two profiles are of different devices: /device:TPU:56 before, /device:TPU:43 now
where the time goes in v2:
time: 121 us
  Pallas kernels  113 us (93%)
  local copies, waits for them, and re-layouts  6.44 us (5%)
    pallas_call x1, Pallas kernels, shards(): pl.pallas_call(kernel, out_shape=[token_shape] * 3, in_specs=[anywhere] *...  113 us
    unnamed x9, local copies, waits for them, and re-layouts  4.93 us

profile of v2, /device:TPU:43, one launch (start us, length us, event | category | flops | bytes accessed | tf_op | source)
XLA Modules:
  0.0 120.6 jit_solution(15337669786351465149)
XLA Ops:
  0.7 0.7 broadcast_compare_fusion.1
  1.4 0.0 copy-start.2
  1.4 0.1 pad_dynamic-slice_fusion
  1.5 0.1 reshape.82
  1.6 0.5 copy-done.2
  2.1 0.6 reshape.81.lse_hbm
  2.7 0.7 broadcast_in_dim.2.bias
  3.4 112.8 %shard_map.94 = (bf16[96,4096]{1,0:T(8,128)(2,1)}, bf16[96,4096]{1,0:T(8,128)(2,1)}, bf16[96,4096]{1,0:T(8,128)(2,1)}) custom-call(bf16[96,4096]{1,0:T(8,128)(2,1)} %q_hbm.1, bf16[96,4096]{1,0:T(8,128)(2,1)} %k_hbm.1, bf16[96,4096]{1,0:T(8,128)(2,1)} %v_hbm.1, bf16[96,4096]{1,0:T(8,128)(2,1)} %o_hbm.1, bf16[96,4096]{1,0:T(8,128)(2,1)} %g_hbm.1, ...), custom_call_target="tpu_custom_call" | custom-call | tf_op jit(solution)/shard_map/pallas_call | solution.py:370
  116.2 0.0 copy-start.1
  116.2 2.1 %copy.15 = bf16[96,4096]{1,0:T(8,128)(2,1)} copy(bf16[96,4096]{1,0:T(8,128)(2,1)} %get-tuple-element.8) | data formatting | bytes 1572864
  118.3 0.0 copy-done.1
  118.4 0.0 copy-start
  118.4 0.9 copy.16
  119.2 0.5 copy-done
  119.8 0.9 copy.17
  (3 shorter events, 0.0 us)
Async XLA Ops:
  1.4 0.7 copy-start.2
  116.2 2.1 %copy-start.1 = (bf16[96,4096]{1,0:T(8,128)(2,1)S(1)}, bf16[96,4096]{1,0:T(8,128)(2,1)}, u32[]{:S(2)}) copy-start(bf16[96,4096]{1,0:T(8,128)(2,1)} %get-tuple-element.9) | copy-start | bytes 2359300
  118.4 1.4 %copy-start = (bf16[96,4096]{1,0:T(8,128)(2,1)S(1)}, bf16[96,4096]{1,0:T(8,128)(2,1)}, u32[]{:S(2)}) copy-start(bf16[96,4096]{1,0:T(8,128)(2,1)} %get-tuple-element.10) | copy-start | bytes 2359300

commit v3 on v2

--- a/solution.py
+++ b/solution.py
@@ -25,7 +25,7 @@
 
 
 def kernel(
-    q_hbm, k_hbm, v_hbm, o_hbm, g_hbm, lse_hbm, bias,
+    q_hbm, k_hbm, v_hbm, o_hbm, g_hbm, lse_hbm, listed,
     dq_out, dk_out, dv_out,
     qb, gb, kb, vb, kt, dqt, dka, dva, stat, kept,
     ob, gl, dl_src, dl, ls, part_src, part, oq, ok, ov,
@@ -170,8 +170,9 @@
             cols = slice((t % 4) * HD, (t % 4 + 1) * HD)
             lse = ls[s, t : t + 1, :] * LOG2E
             stat[s, t // 4, 0:1, cols] = lse
-            stat[s, t // 4, 2:3, cols] = lse + bias[s, 0, t : t + 1, :]
-            stat[s, t // 4, 3:4, cols] = lse + bias[s, 1, t : t + 1, :]
+            centre = listed[(2 * place - 1 + s) * 12 + t, 13] % 4
+            stat[s, t // 4, 2:3, cols] = lse + jnp.where(centre == 2, 1e30, 0.0)
+            stat[s, t // 4, 3:4, cols] = lse + jnp.where(centre == 1, 1e30, 0.0)
 
     def delta_stats(s):
         deltas = []
@@ -354,23 +355,16 @@
 
 
 def shards(queries, key_tokens, value_tokens, outputs, out_grad, log_sum, neighbours):
-    tm, hd = lax.axis_index("tm"), lax.axis_index("head")
-    place = 2 * (1 - tm // 4) + hd % 2
     lse_rows = log_sum.T.reshape(2, 12, HD)
-    centre = neighbours[:, 13] % 4
-    hide = jnp.stack([centre == 2, centre == 1]).astype(jnp.float32) * 1e30
-    hide = jnp.pad(hide, ((0, 0), (12, 12)))
-    hide = lax.dynamic_slice_in_dim(hide, 24 * place, 48, 1).reshape(2, 4, 12)
-    bias = jnp.broadcast_to(hide.transpose(1, 0, 2)[..., None], (4, 2, 12, HD))
     bf16, f32 = jnp.bfloat16, jnp.float32
-    anywhere, vmem = pl.BlockSpec(memory_space=pl.ANY), pl.BlockSpec(memory_space=pltpu.VMEM)
+    anywhere = pl.BlockSpec(memory_space=pl.ANY)
     dma = pltpu.SemaphoreType.DMA
     token_shape = jax.ShapeDtypeStruct(queries.shape, bf16)
     return tuple(
         pl.pallas_call(
             kernel,
             out_shape=[token_shape] * 3,
-            in_specs=[anywhere] * 6 + [vmem],
+            in_specs=[anywhere] * 6 + [pl.BlockSpec(memory_space=pltpu.SMEM)],
             out_specs=[anywhere] * 3,
             scratch_shapes=[
                 pltpu.VMEM((4 * FRAME, HD), bf16),
@@ -406,7 +400,7 @@
             compiler_params=pltpu.CompilerParams(
                 collective_id=0, has_side_effects=True, vmem_limit_bytes=67043328
             ),
-        )(queries, key_tokens, value_tokens, outputs, out_grad, lse_rows, bias)
+        )(queries, key_tokens, value_tokens, outputs, out_grad, lse_rows, neighbours)
     )
 
 

time: 121 us -> 121 us (level)
    unnamed x9 -> x10, local copies, waits for them, and re-layouts: 4.93 us -> 5.16 us
where the time goes in v3:
time: 121 us
  Pallas kernels  114 us (94%)
  local copies, waits for them, and re-layouts  6.49 us (5%)
    pallas_call x1, Pallas kernels, shards(): pl.pallas_call(kernel, out_shape=[token_shape] * 3, in_specs=[anywhere] *...  114 us
    unnamed x10, local copies, waits for them, and re-layouts  5.16 us

profile of v3, /device:TPU:43, one launch (start us, length us, event | category | flops | bytes accessed | tf_op | source)
XLA Modules:
  0.0 120.8 jit_solution(1100116870741311653)
XLA Ops:
  0.6 0.0 copy-start.2
  0.6 1.3 %reshape.9.lse_hbm = f32[2,12,128]{2,1,0:T(8,128)} reshape(f32[2,1536]{1,0:T(2,128)} %bitcast.1) | data formatting | bytes 24576 | tf_op jit(solution)/shard_map/reshape | solution.py:358
  2.0 0.0 copy-done.2
  2.0 0.7 copy.11.listed
  2.7 113.7 %shard_map.94 = (bf16[96,4096]{1,0:T(8,128)(2,1)}, bf16[96,4096]{1,0:T(8,128)(2,1)}, bf16[96,4096]{1,0:T(8,128)(2,1)}) custom-call(bf16[96,4096]{1,0:T(8,128)(2,1)} %q_hbm.1, bf16[96,4096]{1,0:T(8,128)(2,1)} %k_hbm.1, bf16[96,4096]{1,0:T(8,128)(2,1)} %v_hbm.1, bf16[96,4096]{1,0:T(8,128)(2,1)} %o_hbm.1, bf16[96,4096]{1,0:T(8,128)(2,1)} %g_hbm.1, ...), custom_call_target="tpu_custom_call" | custom-call | tf_op jit(solution)/shard_map/pallas_call | solution.py:364
  116.4 0.0 copy-start.1
  116.4 2.1 %copy.15 = bf16[96,4096]{1,0:T(8,128)(2,1)} copy(bf16[96,4096]{1,0:T(8,128)(2,1)} %get-tuple-element.6) | data formatting | bytes 1572864
  118.5 0.0 copy-done.1
  118.5 0.0 copy-start
  118.5 0.9 copy.16
  119.4 0.5 copy-done
  119.9 0.9 copy.17
Async XLA Ops:
  0.6 1.3 %copy-start.2 = (s32[96,27]{0,1:T(8,128)S(1)}, s32[96,27]{0,1:T(8,128)}, u32[]{:S(2)}) copy-start(s32[96,27]{0,1:T(8,128)} %param.13) | copy-start | bytes 31108
  116.4 2.1 %copy-start.1 = (bf16[96,4096]{1,0:T(8,128)(2,1)S(1)}, bf16[96,4096]{1,0:T(8,128)(2,1)}, u32[]{:S(2)}) copy-start(bf16[96,4096]{1,0:T(8,128)(2,1)} %get-tuple-element.7) | copy-start | bytes 2359300
  118.5 1.4 %copy-start = (bf16[96,4096]{1,0:T(8,128)(2,1)S(1)}, bf16[96,4096]{1,0:T(8,128)(2,1)}, u32[]{:S(2)}) copy-start(bf16[96,4096]{1,0:T(8,128)(2,1)} %get-tuple-element.8) | copy-start | bytes 2359300
